TPU v7x, 256 devices: a whole 4x4x8 slice. The times are simulated.
256 devices in a mesh: row: 16 (over x_hi, z), blk: 16 (over x_lo, y, core).
Axes of the slice: x: 4 (x_hi: 2, x_lo: 2; x = x_hi * 2 + x_lo), y: 4, z: 8, core: 2. Of those that a mesh axis runs over, the one named last changes fastest.
Arguments:
- source_table: bfloat16 [8192, 512], P('blk'), may hold values from -6 to 6
- target_table: bfloat16 [131072, 512], P(('row', 'blk')), may hold values from -6 to 6
- message_weight: bfloat16 [512, 512], replicated, may hold values from -0.25 to 0.25
- self_weight: bfloat16 [512, 512], replicated, may hold values from -0.25 to 0.25
- tile_lists: int32 [256, 16], P(('row', 'blk')), may hold values from 0 to 15, each once within a row
- key_offsets: int32 [131072, 16], P(('row', 'blk')), may hold values from 0 to 511
- list_lengths: int32 [256], P(('row', 'blk')), may hold values from 1 to 16, 2048 in all
- cotangent: bfloat16 [131072, 512], P(('row', 'blk')), may hold values from -6 to 6
Outputs:
- updated: bfloat16 [131072, 512], P(('row', 'blk'))
- target_gradient: bfloat16 [131072, 512], P(('row', 'blk'))
- source_gradient: bfloat16 [8192, 512], P(('blk', 'row'))
- self_gradient: float32 [512, 512], replicated
- message_gradient: float32 [512, 512], replicated
Inputs may be any that keep to these rules, and one draw needn't show every extreme that they name: Each row of tile_lists names every one of the 16 source tiles once. A target tile uses the first list_lengths entries of its row of tile_lists.
All inputs are finite; a program needn't handle non-finite values. No bound on the sum of `list_lengths` on one device may be relied on, other than what follows from the above.
Results may differ from a plain program's by a relative error of at most 0.0058.
Values may be sent and summed in bfloat16 or wider, within the bound.
A program may use at most 64 MiB of HBM per device.

v0:
```python
import jax
import jax.numpy as jnp
from jax import lax
from jax.sharding import PartitionSpec as P


def slot_table(lists):
    slot_count = lists.shape[1]
    slot_ids = lax.iota(jnp.int32, slot_count)
    matches = lists[:, :, None] == slot_ids[None, None, :]
    return jnp.sum(jnp.where(matches, slot_ids[None, :, None], 0), axis=1)


def tile_patterns(offset_tiles, slot_column, lengths, tile_rows):
    slot_count = offset_tiles.shape[2]
    chosen_slot = lax.iota(jnp.int32, slot_count)[None, None, :] == slot_column[:, None, None]
    chosen = jnp.sum(jnp.where(chosen_slot, offset_tiles, 0), axis=2)
    used = slot_column < lengths
    positions = lax.iota(jnp.int32, tile_rows)
    pattern = (chosen[:, :, None] == positions[None, None, :]) & used[:, None, None]
    return pattern.astype(jnp.bfloat16)


def local(
    source_table,
    target_table,
    message_weight,
    self_weight,
    tile_lists,
    key_offsets,
    list_lengths,
    cotangent,
):
    tile_rows = target_table.shape[0] // tile_lists.shape[0]
    tiles_here = tile_lists.shape[0]
    slot_count = tile_lists.shape[1]
    width = target_table.shape[1]
    block_rows = source_table.shape[0]
    row_devices = lax.axis_size("row")
    share_rows = block_rows // row_devices
    own_rows = lax.dynamic_slice_in_dim(
        source_table, lax.axis_index("row") * share_rows, share_rows, 0
    )
    projected = jnp.dot(source_table, message_weight, preferred_element_type=jnp.float32).astype(
        jnp.bfloat16
    )
    inverse_tile = 1.0 / list_lengths.astype(jnp.float32)
    slot_of = slot_table(tile_lists)
    offset_tiles = key_offsets.reshape(tiles_here, tile_rows, slot_count)
    start_sum = jnp.zeros((target_table.shape[0], width), jnp.float32)
    pieces = lax.all_gather(projected, "blk", axis=0, tiled=True)
    piece_tiles = pieces.shape[0] // tile_rows

    def gather_visit(local_tile, running):
        source_tile = lax.dynamic_slice_in_dim(pieces, local_tile * tile_rows, tile_rows, 0)
        slot_column = lax.dynamic_index_in_dim(slot_of, local_tile, 1, keepdims=False)
        pattern = tile_patterns(offset_tiles, slot_column, list_lengths, tile_rows)
        added = jnp.einsum("trc,cw->trw", pattern, source_tile, preferred_element_type=jnp.float32)
        return running + added.reshape(running.shape)

    gathered = lax.fori_loop(0, piece_tiles, gather_visit, start_sum)
    inverse_row = jnp.repeat(inverse_tile, tile_rows)[:, None]
    preact = (
        jnp.dot(target_table, self_weight, preferred_element_type=jnp.float32)
        + gathered * inverse_row
    )
    sigmoid_pre = jax.nn.sigmoid(preact)
    updated = (target_table.astype(jnp.float32) + preact * sigmoid_pre).astype(jnp.bfloat16)
    upstream = cotangent.astype(jnp.float32)
    grad_pre = (upstream * sigmoid_pre * (1.0 + preact * (1.0 - sigmoid_pre))).astype(jnp.bfloat16)
    target_gradient = (
        upstream + jnp.dot(grad_pre, self_weight.T, preferred_element_type=jnp.float32)
    ).astype(jnp.bfloat16)
    grad_tiles = grad_pre.reshape(tiles_here, tile_rows, width)

    def tile_terms(slot_column, offsets, lengths, inverses, grads):
        pattern = tile_patterns(offsets, slot_column, lengths, tile_rows)
        terms = jnp.einsum("trc,trw->tcw", pattern, grads, preferred_element_type=jnp.float32)
        return jnp.sum(terms * inverses[:, None, None], axis=0)

    def partial_visit(local_tile, running):
        slot_column = lax.dynamic_index_in_dim(slot_of, local_tile, 1, keepdims=False)
        term = tile_terms(slot_column, offset_tiles, list_lengths, inverse_tile, grad_tiles)
        return lax.dynamic_update_slice_in_dim(running, term, local_tile * tile_rows, 0)

    block_sum = lax.psum_scatter(
        lax.fori_loop(
            0,
            block_rows * lax.axis_size("blk") // tile_rows,
            partial_visit,
            jnp.zeros((block_rows * lax.axis_size("blk"), width), jnp.float32),
        ),
        "blk",
        scatter_dimension=0,
        tiled=True,
    )
    source_sum = lax.psum_scatter(block_sum, "row", scatter_dimension=0, tiled=True)
    source_grad_rounded = source_sum.astype(jnp.bfloat16)
    source_gradient = jnp.dot(
        source_grad_rounded, message_weight.T, preferred_element_type=jnp.float32
    ).astype(jnp.bfloat16)
    self_partial = jnp.dot(target_table.T, grad_pre, preferred_element_type=jnp.float32)
    message_partial = jnp.dot(own_rows.T, source_grad_rounded, preferred_element_type=jnp.float32)
    self_total, message_total = lax.psum((self_partial, message_partial), ("row", "blk"))
    target_total = target_table.shape[0] * row_devices * lax.axis_size("blk")
    source_total = block_rows * lax.axis_size("blk")
    self_gradient = self_total * target_total ** (-0.5)
    message_gradient = message_total * source_total ** (-0.5)
    return (updated, target_gradient, source_gradient, self_gradient, message_gradient)


def solution(mesh):
    placed = (
        P("blk", None),
        P(("row", "blk"), None),
        P(),
        P(),
        P(("row", "blk"), None),
        P(("row", "blk"), None),
        P(("row", "blk")),
        P(("row", "blk"), None),
    )
    return jax.shard_map(
        local,
        mesh=mesh,
        in_specs=placed,
        out_specs=(
            P(("row", "blk"), None),
            P(("row", "blk"), None),
            P(("blk", "row"), None),
            P(),
            P(),
        ),
        check_vma=False,
    )
```

profile of v0, /device:TPU:2, one launch (start us, length us, event | category | flops | bytes accessed | tf_op | source)
XLA Modules:
  0.0 807.8 jit_solution(3190670035176118978)
XLA Ops:
  7.2 2.5 convolution_convert_fusion
  11.2 56.8 %all-gather.2.cloned.1.call-done = bf16[8192,512]{1,0:T(8,128)(2,1)} async-done(((bf16[512,512]{1,0:T(8,128)(2,1)}), bf16[8192,512]{1,0:T(8,128)(2,1)}) %all-gather.2.cloned.1.call-update) | async-done | bytes 8388624 | tf_op jit(solution)/shard_map/all_gather | solution.py:51
  68.0 80.6 %while.28 = (s32[]{:T(128)}, f32[512,512]{1,0:T(8,128)S(1)}, s32[1,16]{1,0:T(1,128)S(1)}, s32[1,512,16]{1,2,0:T(8,128)}, s32[1]{0:T(128)}, /*index=5*/bf16[8192,...) while((s32[]{:T(128)}, f32[512,512]{1,0:T(8,128)S(1)}, s32[1,16]{1,0:T(1,128)S(1)}, ...), condition=%wide.region_3.4_spmd.clone, body=%wide.region_1.3_spmd.clone.sunk | while | flops 269499936 | bytes 2659034 | solution.py:61
  69.2 0.8 select_reduce_fusion.6
  71.4 1.6 convolution_add_fusion.4
  74.3 0.8 select_reduce_fusion.6
  76.4 1.6 convolution_add_fusion.4
  79.3 0.8 select_reduce_fusion.6
  81.5 1.6 convolution_add_fusion.4
  84.4 0.8 select_reduce_fusion.6
  86.5 1.6 convolution_add_fusion.4
  89.4 0.8 select_reduce_fusion.6
  91.6 1.6 convolution_add_fusion.4
  94.4 0.8 select_reduce_fusion.6
  96.6 1.6 convolution_add_fusion.4
  99.5 0.8 select_reduce_fusion.6
  101.6 1.6 convolution_add_fusion.4
  104.5 0.8 select_reduce_fusion.6
  106.7 1.6 convolution_add_fusion.4
  109.6 0.8 select_reduce_fusion.6
  111.7 1.6 convolution_add_fusion.4
  114.6 0.8 select_reduce_fusion.6
  116.8 1.6 convolution_add_fusion.4
  119.7 0.8 select_reduce_fusion.6
  121.8 1.6 convolution_add_fusion.4
  124.7 0.8 select_reduce_fusion.6
  126.8 1.6 convolution_add_fusion.4
  129.7 0.8 select_reduce_fusion.6
  131.9 1.6 convolution_add_fusion.4
  134.8 0.8 select_reduce_fusion.6
  136.9 1.6 convolution_add_fusion.4
  139.8 0.8 select_reduce_fusion.6
  142.0 1.6 convolution_add_fusion.4
  144.9 0.8 select_reduce_fusion.6
  147.0 1.6 convolution_add_fusion.4
  148.7 3.0 fusion.15
  151.7 7.9 broadcast_in_dim.94
  159.6 67.2 %while.27 = (s32[]{:T(128)}, f32[8192,512]{1,0:T(8,128)}, s32[1,16]{1,0:T(1,128)S(1)}, s32[1,512,16]{1,2,0:T(8,128)S(1)}, s32[1]{0:T(128)}, /*index=5*/bf16[1,51...) while((s32[]{:T(128)}, f32[8192,512]{1,0:T(8,128)}, ...), condition=%wide.region_6.7_spmd, body=%wide.region_4.6_spmd.sunk | while | flops 269237792 | bytes 1610968 | solution.py:87
  162.2 1.5 fusion.37
  166.4 1.6 fusion.37
  170.6 1.6 fusion.37
  174.8 1.6 fusion.37
  179.0 1.6 fusion.37
  183.2 1.6 fusion.37
  187.4 1.6 fusion.37
  191.6 1.6 fusion.37
  195.8 1.6 fusion.37
  200.0 1.5 fusion.37
  204.2 1.6 fusion.37
  208.4 1.6 fusion.37
  212.6 1.6 fusion.37
  216.8 1.5 fusion.37
  221.0 1.6 fusion.37
  225.2 1.6 fusion.37
  226.8 101.1 %reduce-scatter.3.cloned.1.call-done = f32[512,512]{1,0:T(8,128)} async-done(((f32[8192,512]{1,0:T(8,128)}), f32[512,512]{1,0:T(8,128)}) %reduce-scatter.3.cloned.1.call-update) | async-done | bytes 1048592 | tf_op jit(solution)/shard_map/reduce_scatter | solution.py:86
  328.0 1.4 convolution_bitcast_fusion
  329.4 200.2 %reduce-scatter.5.cloned.1.call-done = f32[32,512]{1,0:T(8,128)} async-done(((f32[512,512]{1,0:T(8,128)}), f32[32,512]{1,0:T(8,128)}) %reduce-scatter.5.cloned.1.call-update) | async-done | bytes 65552 | tf_op jit(solution)/shard_map/reduce_scatter | solution.py:97
  529.6 2.1 fusion.16
  531.8 1.3 fusion.13
  533.1 1.7 convolution_convert_fusion.1
  534.8 261.5 %all-reduce.3.cloned.1.call-done = (f32[512,512]{0,1:T(8,128)}, f32[512,512]{1,0:T(8,128)}) async-done(((f32[512,512]{0,1:T(8,128)}, f32[512,512]{1,0:T(8,128)}), (f32[512,512]{0,1:T(8,128)}, f32[512,512]{1,0:T(8,128)})) %all-reduce.3.cloned.1.call-update) | async-done | bytes 2097168 | tf_op jit(solution)/shard_map/psum | solution.py:104
  796.3 1.3 broadcast_multiply_fusion.1
  797.7 1.3 copy.15
  799.0 2.3 broadcast_multiply_fusion
  (100 shorter events, 41.9 us)
Async XLA Ops:
  7.2 141.5 %copy-start = (bf16[512,512]{1,0:T(8,128)(2,1)S(1)}, bf16[512,512]{1,0:T(8,128)(2,1)}, u32[]{:S(2)}) copy-start(bf16[512,512]{1,0:T(8,128)(2,1)} %param.15) | copy-start | bytes 1572868
  7.2 60.8 %all-gather.2.cloned.1.call-start = ((), (), s32[]{:S(2)}) async-start(), calls=%async_computation.2 | async-start | bytes 8912896 | tf_op jit(solution)/shard_map/all_gather | solution.py:51
  9.7 318.2 %reduce-scatter.3.cloned.1.call-start = ((), (), s32[]{:S(2)}) async-start(), calls=%async_computation.3 | async-start | bytes 17825792 | tf_op jit(solution)/shard_map/reduce_scatter | solution.py:86
  148.6 10.9 %copy-start.1 = (s32[1,512,16]{1,2,0:T(8,128)S(1)}, s32[1,512,16]{1,2,0:T(8,128)}, u32[]{:S(2)}) copy-start(s32[1,512,16]{1,2,0:T(8,128)} %get-tuple-element.461) | copy-start | bytes 98308
  159.6 168.4 %copy-start.3 = (bf16[512,512]{1,0:T(8,128)(2,1)S(1)}, bf16[512,512]{1,0:T(8,128)(2,1)}, u32[]{:S(2)}) copy-start(bf16[512,512]{1,0:T(8,128)(2,1)} %param.13) | copy-start | bytes 1572868
  159.6 372.2 %copy-start.4 = (bf16[512,512]{1,0:T(8,128)(2,1)S(1)}, bf16[512,512]{1,0:T(8,128)(2,1)}, u32[]{:S(2)}) copy-start(bf16[512,512]{1,0:T(8,128)(2,1)} %param.19) | copy-start | bytes 1572868
  159.6 373.5 %copy-start.2 = (bf16[512,512]{1,0:T(8,128)(2,1)S(1)}, bf16[512,512]{1,0:T(8,128)(2,1)}, u32[]{:S(2)}) copy-start(bf16[512,512]{1,0:T(8,128)(2,1)} %param.14) | copy-start | bytes 1572868
  226.8 302.9 %reduce-scatter.5.cloned.1.call-start = ((), (), s32[]{:S(2)}) async-start(), calls=%async_computation.4 | async-start | bytes 1114112 | tf_op jit(solution)/shard_map/reduce_scatter | solution.py:97
  327.9 468.4 %all-reduce.3.cloned.1.call-start = ((), (), s32[]{:S(2)}) async-start(), calls=%async_computation.5 | async-start | bytes 4194304 | tf_op jit(solution)/shard_map/psum | solution.py:104
Sparse Core Ops, SparseCore 0:
  10.4 57.5 all-gather.1
  226.9 100.9 reduce-scatter.2
  331.7 197.8 reduce-scatter.4
  535.6 260.6 all-reduce.2
where the time goes:
time: 811 us; the launch traced here: 808 us
  waiting for transfers between devices  620 us (76%)
  matrix products  63 us (8%)
  loops' own time  42.4 us (5%)
  other arithmetic  40.2 us (5%)
  local copies, waits for them, and re-layouts  27.9 us (3%)
  between operations  14.5 us (2%)
    psum x1, waiting for transfers between devices, local(): lax.psum((self_partial, message_partial), ('row', 'blk'))  262 us
    reduce_scatter x1, waiting for transfers between devices, local(): lax.psum_scatter(block_sum, 'row', scatter_dimension=0, tiled=True)  200 us
    reduce_scatter x1, waiting for transfers between devices, local(): lax.psum_scatter(lax.fori_loop(0, block_rows * lax.axis_size('blk') // ti...  101 us
    all_gather x1, waiting for transfers between devices, local(): pieces = lax.all_gather(projected, 'blk', axis=0, tiled=True)  56.8 us
    dot_general x16, matrix products, gather_visit(): jnp.einsum('trc,cw->trw', pattern, source_tile, preferred_element_type=jn...  25.9 us
    dot_general x16, matrix products, tile_terms(): jnp.einsum('trc,trw->tcw', pattern, grads, preferred_element_type=jnp.flo...  25.1 us
    another operation x1, loops' own time, local(): gathered = lax.fori_loop(0, piece_tiles, gather_visit, start_sum)  21.4 us
    another operation x1, loops' own time, local(): lax.fori_loop(0, block_rows * lax.axis_size('blk') // tile_rows, partial_...  21 us
  transfers between devices with their start and end apart: 4, of which 4 were waited for; matrix products, arithmetic and copies ran while one was open for 1% of the time, Pallas kernels for 0%

commit v1 on v0

--- a/solution.py
+++ b/solution.py
@@ -101,7 +101,7 @@
     ).astype(jnp.bfloat16)
     self_partial = jnp.dot(target_table.T, grad_pre, preferred_element_type=jnp.float32)
     message_partial = jnp.dot(own_rows.T, source_grad_rounded, preferred_element_type=jnp.float32)
-    self_total, message_total = lax.psum((self_partial, message_partial), ("row", "blk"))
+    self_total, message_total = lax.psum(lax.psum((self_partial, message_partial), "row"), "blk")
     target_total = target_table.shape[0] * row_devices * lax.axis_size("blk")
     source_total = block_rows * lax.axis_size("blk")
     self_gradient = self_total * target_total ** (-0.5)

time: 811 us -> 838 us (1.033)
  waiting for transfers between devices: 620 us -> 646 us
    psum x1 -> x2, waiting for transfers between devices: 262 us -> 288 us  [the longest x1 162 us: local(): lax.psum((self_partial, message_partial), 'row')]
  transfers between devices with their start and end apart: 4 -> 5, of which waited for: 4 -> 5; matrix products, arithmetic and copies ran while one was open for 1% -> 1% of each run, Pallas kernels for 0% -> 0%
where the time goes in v1:
time: 838 us; the launch traced here: 834 us
  waiting for transfers between devices  646 us (77%)
  matrix products  63.2 us (8%)
  loops' own time  42.4 us (5%)
  other arithmetic  40.2 us (5%)
  local copies, waits for them, and re-layouts  27.9 us (3%)
  between operations  14.5 us (2%)
    reduce_scatter x1, waiting for transfers between devices, local(): lax.psum_scatter(block_sum, 'row', scatter_dimension=0, tiled=True)  200 us
    psum x1, waiting for transfers between devices, local(): lax.psum((self_partial, message_partial), 'row')  162 us
    psum x1, waiting for transfers between devices, local(): lax.psum(lax.psum((self_partial, message_partial), 'row'), 'blk')  125 us
    reduce_scatter x1, waiting for transfers between devices, local(): lax.psum_scatter(lax.fori_loop(0, block_rows * lax.axis_size('blk') // ti...  101 us
    all_gather x1, waiting for transfers between devices, local(): pieces = lax.all_gather(projected, 'blk', axis=0, tiled=True)  56.8 us
    dot_general x16, matrix products, gather_visit(): jnp.einsum('trc,cw->trw', pattern, source_tile, preferred_element_type=jn...  25.9 us
    dot_general x16, matrix products, tile_terms(): jnp.einsum('trc,trw->tcw', pattern, grads, preferred_element_type=jnp.flo...  25.2 us
    another operation x1, loops' own time, local(): gathered = lax.fori_loop(0, piece_tiles, gather_visit, start_sum)  21.4 us
  transfers between devices with their start and end apart: 5, of which 5 were waited for; matrix products, arithmetic and copies ran while one was open for 1% of the time, Pallas kernels for 0%

profile of v1, /device:TPU:2, one launch (start us, length us, event | category | flops | bytes accessed | tf_op | source)
XLA Modules:
  0.0 834.0 jit_solution(7665570716639026627)
XLA Ops:
  7.2 2.5 convolution_convert_fusion
  11.2 56.8 %all-gather.2.cloned.1.call-done = bf16[8192,512]{1,0:T(8,128)(2,1)} async-done(((bf16[512,512]{1,0:T(8,128)(2,1)}), bf16[8192,512]{1,0:T(8,128)(2,1)}) %all-gather.2.cloned.1.call-update) | async-done | bytes 8388624 | tf_op jit(solution)/shard_map/all_gather | solution.py:51
  68.0 80.6 %while.28 = (s32[]{:T(128)}, f32[512,512]{1,0:T(8,128)S(1)}, s32[1,16]{1,0:T(1,128)S(1)}, s32[1,512,16]{1,2,0:T(8,128)}, s32[1]{0:T(128)}, /*index=5*/bf16[8192,...) while((s32[]{:T(128)}, f32[512,512]{1,0:T(8,128)S(1)}, s32[1,16]{1,0:T(1,128)S(1)}, ...), condition=%wide.region_3.4_spmd.clone, body=%wide.region_1.3_spmd.clone.sunk | while | flops 269499936 | bytes 2659034 | solution.py:61
  69.2 0.8 select_reduce_fusion.6
  71.4 1.6 convolution_add_fusion.4
  74.3 0.8 select_reduce_fusion.6
  76.4 1.6 convolution_add_fusion.4
  79.3 0.8 select_reduce_fusion.6
  81.5 1.6 convolution_add_fusion.4
  84.4 0.8 select_reduce_fusion.6
  86.5 1.6 convolution_add_fusion.4
  89.4 0.8 select_reduce_fusion.6
  91.6 1.6 convolution_add_fusion.4
  94.4 0.8 select_reduce_fusion.6
  96.6 1.6 convolution_add_fusion.4
  99.5 0.8 select_reduce_fusion.6
  101.6 1.6 convolution_add_fusion.4
  104.5 0.8 select_reduce_fusion.6
  106.7 1.6 convolution_add_fusion.4
  109.6 0.8 select_reduce_fusion.6
  111.7 1.6 convolution_add_fusion.4
  114.6 0.8 select_reduce_fusion.6
  116.8 1.6 convolution_add_fusion.4
  119.7 0.8 select_reduce_fusion.6
  121.8 1.6 convolution_add_fusion.4
  126.8 1.6 convolution_add_fusion.4
  129.7 0.8 select_reduce_fusion.6
  131.9 1.6 convolution_add_fusion.4
  134.8 0.8 select_reduce_fusion.6
  136.9 1.6 convolution_add_fusion.4
  139.8 0.8 select_reduce_fusion.6
  142.0 1.6 convolution_add_fusion.4
  144.9 0.8 select_reduce_fusion.6
  147.0 1.6 convolution_add_fusion.4
  148.7 3.0 fusion.15
  151.7 7.9 broadcast_in_dim.94
  159.6 67.3 %while.27 = (s32[]{:T(128)}, f32[8192,512]{1,0:T(8,128)}, s32[1,16]{1,0:T(1,128)S(1)}, s32[1,512,16]{1,2,0:T(8,128)S(1)}, s32[1]{0:T(128)}, /*index=5*/bf16[1,51...) while((s32[]{:T(128)}, f32[8192,512]{1,0:T(8,128)}, ...), condition=%wide.region_6.7_spmd, body=%wide.region_4.6_spmd.sunk | while | flops 269237792 | bytes 1610968 | solution.py:87
  162.2 1.6 fusion.37
  166.4 1.6 fusion.37
  170.7 1.6 fusion.37
  174.9 1.6 fusion.37
  179.1 1.5 fusion.37
  183.2 1.6 fusion.37
  187.5 1.6 fusion.37
  191.7 1.6 fusion.37
  195.9 1.6 fusion.37
  200.1 1.5 fusion.37
  204.3 1.5 fusion.37
  208.5 1.6 fusion.37
  212.7 1.6 fusion.37
  216.9 1.6 fusion.37
  221.1 1.6 fusion.37
  225.3 1.6 fusion.37
  227.0 101.1 %reduce-scatter.3.cloned.1.call-done = f32[512,512]{1,0:T(8,128)} async-done(((f32[8192,512]{1,0:T(8,128)}), f32[512,512]{1,0:T(8,128)}) %reduce-scatter.3.cloned.1.call-update) | async-done | bytes 1048592 | tf_op jit(solution)/shard_map/reduce_scatter | solution.py:86
  328.1 1.4 convolution_bitcast_fusion
  329.6 200.2 %reduce-scatter.5.cloned.1.call-done = f32[32,512]{1,0:T(8,128)} async-done(((f32[512,512]{1,0:T(8,128)}), f32[32,512]{1,0:T(8,128)}) %reduce-scatter.5.cloned.1.call-update) | async-done | bytes 65552 | tf_op jit(solution)/shard_map/reduce_scatter | solution.py:97
  529.8 2.1 fusion.16
  532.0 162.2 %all-reduce.7.cloned.1.call-done = (f32[512,512]{0,1:T(8,128)}, f32[512,512]{1,0:T(8,128)}) async-done(((f32[512,512]{0,1:T(8,128)}, f32[512,512]{1,0:T(8,128)}), (f32[512,512]{0,1:T(8,128)}, f32[512,512]{1,0:T(8,128)})) %all-reduce.7.cloned.1.call-update) | async-done | bytes 2097168 | tf_op jit(solution)/shard_map/psum | solution.py:104
  694.2 1.3 fusion.13
  695.4 1.7 convolution_convert_fusion.1
  697.2 125.4 %all-reduce.5.cloned.1.call-done = (f32[512,512]{0,1:T(8,128)}, f32[512,512]{1,0:T(8,128)}) async-done(((f32[512,512]{0,1:T(8,128)}, f32[512,512]{1,0:T(8,128)}), (f32[512,512]{0,1:T(8,128)}, f32[512,512]{1,0:T(8,128)})) %all-reduce.5.cloned.1.call-update) | async-done | bytes 2097168 | tf_op jit(solution)/shard_map/psum | solution.py:104
  822.5 1.3 broadcast_multiply_fusion.1
  823.9 1.3 copy.15
  825.2 2.3 broadcast_multiply_fusion
  (103 shorter events, 42.8 us)
Async XLA Ops:
  7.2 141.5 %copy-start = (bf16[512,512]{1,0:T(8,128)(2,1)S(1)}, bf16[512,512]{1,0:T(8,128)(2,1)}, u32[]{:S(2)}) copy-start(bf16[512,512]{1,0:T(8,128)(2,1)} %param.15) | copy-start | bytes 1572868
  7.2 60.8 %all-gather.2.cloned.1.call-start = ((), (), s32[]{:S(2)}) async-start(), calls=%async_computation.2 | async-start | bytes 8912896 | tf_op jit(solution)/shard_map/all_gather | solution.py:51
  9.7 318.3 %reduce-scatter.3.cloned.1.call-start = ((), (), s32[]{:S(2)}) async-start(), calls=%async_computation.3 | async-start | bytes 17825792 | tf_op jit(solution)/shard_map/reduce_scatter | solution.py:86
  148.6 10.9 %copy-start.1 = (s32[1,512,16]{1,2,0:T(8,128)S(1)}, s32[1,512,16]{1,2,0:T(8,128)}, u32[]{:S(2)}) copy-start(s32[1,512,16]{1,2,0:T(8,128)} %get-tuple-element.467) | copy-start | bytes 98308
  159.6 168.5 %copy-start.3 = (bf16[512,512]{1,0:T(8,128)(2,1)S(1)}, bf16[512,512]{1,0:T(8,128)(2,1)}, u32[]{:S(2)}) copy-start(bf16[512,512]{1,0:T(8,128)(2,1)} %param.13) | copy-start | bytes 1572868
  159.6 534.6 %copy-start.4 = (bf16[512,512]{1,0:T(8,128)(2,1)S(1)}, bf16[512,512]{1,0:T(8,128)(2,1)}, u32[]{:S(2)}) copy-start(bf16[512,512]{1,0:T(8,128)(2,1)} %param.19) | copy-start | bytes 1572868
  159.6 535.9 %copy-start.2 = (bf16[512,512]{1,0:T(8,128)(2,1)S(1)}, bf16[512,512]{1,0:T(8,128)(2,1)}, u32[]{:S(2)}) copy-start(bf16[512,512]{1,0:T(8,128)(2,1)} %param.14) | copy-start | bytes 1572868
  226.9 302.8 %reduce-scatter.5.cloned.1.call-start = ((), (), s32[]{:S(2)}) async-start(), calls=%async_computation.4 | async-start | bytes 1114112 | tf_op jit(solution)/shard_map/reduce_scatter | solution.py:97
  328.1 366.1 %all-reduce.7.cloned.1.call-start = ((), (), s32[]{:S(2)}) async-start(), calls=%async_computation.6 | async-start | bytes 4194304 | tf_op jit(solution)/shard_map/psum | solution.py:104
  531.9 290.6 %all-reduce.5.cloned.1.call-start = ((), (), s32[]{:S(2)}) async-start(), calls=%async_computation.5 | async-start | bytes 4194304 | tf_op jit(solution)/shard_map/psum | solution.py:104
Sparse Core Ops, SparseCore 0:
  10.4 57.5 all-gather.1
  227.0 100.9 reduce-scatter.2
  331.9 197.8 reduce-scatter.4
  532.9 161.2 all-reduce.6
  696.7 125.8 all-reduce.4
